TPU v7x, 32 devices: a whole 2x2x4 slice. The times are simulated.
32 devices in a mesh: space: 16 (over z, y, core), bead: 2 (over x).
Axes of the slice: x: 2, y: 2, z: 4, core: 2. Of those that a mesh axis runs over, the one named last changes fastest.
Arguments:
- centroids: float32 [3, 4096], P(None, 'space'), may hold values from 0 to 1
- offsets: float32 [3, 8, 4096], P(None, 'bead', 'space'), may hold values from -1 to 1
- velocities: float32 [3, 8, 4096], P(None, 'bead', 'space'), may hold values from -12 to 12
- charges: float32 [4096], P('space'), may hold values from -3 to 3
- polar: float32 [4096], P('space'), may hold values from 0.4 to 1.6
- masses: float32 [4096], P('space'), may hold values from 1 to 16
- groups: int32 [4096], P('space'), may hold values from 0 to 2047, never falling along the last dimension, each value on 1 to 3 neighbouring positions
- tiles: int32 [32, 4], P('space'), may hold values from 0 to 5, as said below
Outputs:
- dipoles: float32 [3, 8, 4096], P(None, 'bead', 'space')
- forces: float32 [3, 8, 4096], P(None, 'bead', 'space')
- new_velocity: float32 [3, 8, 4096], P(None, 'bead', 'space')
- new_offset: float32 [3, 8, 4096], P(None, 'bead', 'space')
Inputs may be any that keep to these rules, and one draw needn't show every extreme that they name: `tiles`: row c lists 4 different blocks, numbered within the concatenation of the slab before block c's slab (periodically), block c's own slab and the slab after, each of 2 blocks of 128 consecutive atoms.
All inputs are finite; a program needn't handle non-finite values.
Results may differ from a plain program's by a relative error of at most 0.0004.
Values sent between devices are 32-bit elements; how exact they have to be, the bound alone decides.
A program may use at most 64 MiB of HBM per device.

v0:
```python
import jax
import jax.numpy as jnp
from jax import lax
from jax.sharding import PartitionSpec as P

BLOCK = 128
NT = 4
ITERS = 3


slab_width = 9.0
box_side = 24.0
cut_square = 64.0
thole_coef = 0.39
bond_coef = 4.0
time_step = 0.05
target_temp = 8.0
coupling = 0.5


def extended(array, sides, width):
    for axis, dim in sides:
        count, length = (lax.axis_size(axis), array.shape[dim])
        up = [(i, (i + 1) % count) for i in range(count)]
        down = [(j, i) for i, j in up]
        last = lax.slice_in_dim(array, length - width, length, axis=dim)
        first = lax.slice_in_dim(array, 0, width, axis=dim)
        before = lax.ppermute(last, axis, up)
        after = lax.ppermute(first, axis, down)
        array = jnp.concatenate([before, array, after], axis=dim)
    return array


def shifted(array, axis, by):
    count = lax.axis_size(axis)
    return lax.ppermute(array, axis, [(i, (i + by) % count) for i in range(count)])


def geometry(xi, ai, gi, xj, aj, gj, keep, period):
    delta = xi[:, :, :, None] - xj[:, :, None, :]
    delta = delta - period * jnp.floor(delta / period + 0.5)
    square = jnp.sum(delta * delta, axis=0) + 1.0
    damp = thole_coef * square * jnp.sqrt(square) / jnp.sqrt(ai[:, None] * aj[None, :])
    fade = jnp.exp(-damp)
    lam_three = 1.0 - fade
    lam_five = 1.0 - (1.0 + damp) * fade
    taper = jnp.where(square < cut_square, (1.0 - square / cut_square) ** 2, 0.0)
    weight = taper * jnp.where(gi[:, None] == gj[None, :], 0.0, 1.0) * keep[None, :]
    inv_three = weight * lam_three / (square * jnp.sqrt(square))
    inv_five = 3.0 * weight * lam_five / (square * square * jnp.sqrt(square))
    return (delta, inv_three, inv_five)


def permanent(xi, ai, gi, xj, qj, aj, gj, keep, period):
    delta, inv_three, inv_five = geometry(xi, ai, gi, xj, aj, gj, keep, period)
    return jnp.sum(delta * (inv_three * qj[None, :])[None], axis=-1)


def mutual(xi, ai, gi, xj, aj, gj, muj, keep, period):
    delta, inv_three, inv_five = geometry(xi, ai, gi, xj, aj, gj, keep, period)
    along = jnp.sum(delta * muj[:, :, None, :], axis=0)
    return jnp.sum(delta * (inv_five * along)[None], axis=-1) - jnp.sum(
        inv_three[None] * muj[:, :, None, :], axis=-1
    )


def energy(xi, xj, ai, gi, qj, aj, gj, mui, muj, keep, period):
    first = permanent(xi, ai, gi, xj, qj, aj, gj, keep, period)
    second = mutual(xi, ai, gi, xj, aj, gj, muj, keep, period)
    return -jnp.sum(mui * (first + 0.5 * second))


def neighbour_dipoles(mu, width):
    return extended(mu, (("space", 2),), width)


def per_device(centroids, offsets, velocities, charges, polar, masses, groups, tiles):
    nspace = lax.axis_size("space")
    slab = lax.axis_index("space").astype(jnp.float32)
    atoms_dev = centroids.shape[1]
    beads_dev = offsets.shape[1]
    nblk = atoms_dev // BLOCK
    base = jnp.stack(
        [(slab + centroids[0]) * slab_width, centroids[1] * box_side, centroids[2] * box_side]
    )
    positions = base[:, None, :] + offsets
    props = jnp.stack([charges, polar, groups.astype(jnp.float32)])[:, None, :]
    ext_pos, ext_props = (
        extended(positions, (("space", 2),), atoms_dev),
        extended(props, (("space", 2),), atoms_dev),
    )
    period = jnp.array([nspace * slab_width, box_side, box_side], jnp.float32).reshape(3, 1, 1, 1)
    keep = jnp.ones((NT * BLOCK,), jnp.float32)
    pos_b = positions.reshape(3, beads_dev, nblk, BLOCK)
    ext_b = ext_pos.reshape(3, beads_dev, 3 * nblk, BLOCK)
    ext_q = ext_props[0, 0].reshape(3 * nblk, BLOCK)
    ext_a = ext_props[1, 0].reshape(3 * nblk, BLOCK)
    ext_g = ext_props[2, 0].reshape(3 * nblk, BLOCK)
    own_a = polar.reshape(nblk, BLOCK)
    own_g = ext_g[nblk : 2 * nblk]
    order = jnp.arange(nblk, dtype=jnp.int32)

    def spread(field):
        return jnp.moveaxis(field, 0, 2).reshape(3, -1, atoms_dev)

    def perm_block(b):
        src = tiles[b]
        return permanent(
            pos_b[:, :, b],
            own_a[b],
            own_g[b],
            ext_b[:, :, src].reshape(3, beads_dev, -1),
            ext_q[src].reshape(-1),
            ext_a[src].reshape(-1),
            ext_g[src].reshape(-1),
            keep,
            period,
        )

    field0 = spread(lax.map(perm_block, order))
    mu = polar * field0
    for step in range(ITERS):
        count = beads_dev - 0
        mu_b = neighbour_dipoles(mu, atoms_dev).reshape(3, count, 3 * nblk, BLOCK)

        def one(b):
            src = tiles[b]
            return mutual(
                pos_b[:, :, b],
                own_a[b],
                own_g[b],
                ext_b[:, :, src].reshape(3, count, -1),
                ext_a[src].reshape(-1),
                ext_g[src].reshape(-1),
                mu_b[:, :, src].reshape(3, count, -1),
                keep,
                period,
            )

        mu = polar * (field0 + spread(lax.map(one, order)))
    ext_mu = neighbour_dipoles(mu, atoms_dev)
    ext_mu = ext_mu.reshape(3, beads_dev, 3 * nblk, BLOCK)
    slope = jax.grad(energy, argnums=(0, 1))

    def grad_block(b):
        src = tiles[b]
        return slope(
            pos_b[:, :, b],
            ext_b[:, :, src].reshape(3, beads_dev, -1),
            own_a[b],
            own_g[b],
            ext_q[src].reshape(-1),
            ext_a[src].reshape(-1),
            ext_g[src].reshape(-1),
            ext_mu[:, :, nblk + b],
            ext_mu[:, :, src].reshape(3, beads_dev, -1),
            keep,
            period,
        )

    own_grad, src_grad = lax.map(grad_block, order)
    onehot = (tiles[:, :, None] == jnp.arange(3 * nblk, dtype=jnp.int32)[None, None, :]).astype(
        jnp.float32
    )
    src_grad = src_grad.reshape(nblk, 3, beads_dev, NT, BLOCK)
    ext_grad = jnp.einsum("ncbtl,nte->cbel", src_grad, onehot, precision=lax.Precision.HIGHEST)
    total = jnp.moveaxis(own_grad, 0, 2) + ext_grad[:, :, nblk : 2 * nblk]
    total = total.reshape(3, beads_dev, atoms_dev)
    left_part = ext_grad[:, :, :nblk].reshape(3, beads_dev, atoms_dev)
    right_part = ext_grad[:, :, 2 * nblk :].reshape(3, beads_dev, atoms_dev)
    total = total + shifted(left_part, "space", -1)
    total = total + shifted(right_part, "space", 1)
    forces = -total
    kinetic_sum = lax.psum(
        jnp.sum(masses[None, None, :] * velocities * velocities), ("space", "bead")
    )
    kinetic = kinetic_sum / (3.0 * atoms_dev * nspace * beads_dev * lax.axis_size("bead"))
    scale = jnp.sqrt(1.0 + coupling * (target_temp / kinetic - 1.0))
    padded_beads = extended(offsets, (("bead", 1),), 1)
    before = padded_beads[:, :-2]
    after = padded_beads[:, 2:]
    restoring = -bond_coef * (2.0 * offsets - before - after)
    new_velocity = scale * velocities + time_step * (forces / masses[None, None, :] + restoring)
    new_offset = offsets + time_step * new_velocity
    return (mu, forces, new_velocity, new_offset)


def solution(mesh):
    placed = (
        P(None, "space"),
        P(None, "bead", "space"),
        P(None, "bead", "space"),
        P("space"),
        P("space"),
        P("space"),
        P("space"),
        P("space", None),
    )
    return jax.shard_map(
        per_device,
        mesh=mesh,
        in_specs=placed,
        out_specs=(
            P(None, "bead", "space"),
            P(None, "bead", "space"),
            P(None, "bead", "space"),
            P(None, "bead", "space"),
        ),
        check_vma=False,
    )
```

profile of v0, /device:TPU:0, one launch (start us, length us, event | category | flops | bytes accessed | tf_op | source)
XLA Modules:
  0.0 224.5 jit_solution(6781361177932330156)
XLA Ops:
  0.6 0.8 add_multiply_fusion
  1.5 0.7 broadcast_add_fusion
  2.7 5.0 %collective-permute-start.1 = (f32[3,4,256]{2,1,0:T(4,128)S(1)}, f32[3,4,256]{2,1,0:T(4,128)S(1)}, u32[]{:S(2)}, u32[]{:S(2)}) collective-permute-start(f32[3,4,256]{2,1,0:T(4,128)S(1)} %broadcast_add_fusion), channel_id=1, source_target_pairs={{2,0},{4,2},{6,4},{8,6},{10,8},{12,10},{14,12},{16,14},{18,16},{20... | collective-permute-start | bytes 36872 | tf_op jit(solution)/shard_map/ppermute | solution.py:29
  8.3 0.7 pad_maximum_fusion.3
  9.1 4.4 %collective-permute-start.3 = (f32[3,1,256]{2,1,0:T(1,128)S(1)}, f32[3,1,256]{2,1,0:T(1,128)S(1)}, u32[]{:S(2)}, u32[]{:S(2)}) collective-permute-start(f32[3,1,256]{2,1,0:T(1,128)S(1)} %broadcast_in_dim.161), channel_id=1, source_target_pairs={{2,0},{4,2},{6,4},{8,6},{10,8},{12,10},{14,12},{16,14},{18,16},{20... | collective-permute-start | bytes 9224 | tf_op jit(solution)/shard_map/ppermute | solution.py:29
  13.5 0.7 fusion.134
  14.9 19.4 %while.59 = (s32[]{:T(128)}, f32[2,3,4,128]{3,2,1,0:T(4,128)S(1)}, s32[2]{0:T(128)S(1)}, f32[3,4,2,128]{3,1,0,2:T(4,128)S(1)}, s32[2,4]{1,0:T(2,128)}, /*index=5...) while((s32[]{:T(128)}, f32[2,3,4,128]{3,2,1,0:T(4,128)S(1)}, ...), condition=%wide.region_3.4_spmd.clone, body=%wide.region_0.3_spmd.clone.sunk | while | flops 16711185 | bytes 5463591 | solution.py:120
  18.8 1.6 fusion.189
  22.4 0.9 fusion.191
  23.3 1.3 fusion.192
  28.5 1.6 fusion.189
  32.1 0.9 fusion.191
  33.0 1.3 fusion.192
  35.0 4.4 %collective-permute-start.5 = (f32[3,4,256]{2,1,0:T(4,128)S(1)}, f32[3,4,256]{2,1,0:T(4,128)S(1)}, u32[]{:S(2)}, u32[]{:S(2)}) collective-permute-start(f32[3,4,256]{2,1,0:T(4,128)S(1)} %bitcast_multiply_fusion), channel_id=1, source_target_pairs={{2,0},{4,2},{6,4},{8,6},{10,8},{12,10},{14,12},{16,14},{18,16},{20... | collective-permute-start | bytes 36872 | tf_op jit(solution)/shard_map/ppermute | solution.py:29
  39.5 1.4 collective-permute-done.4
  40.9 21.8 %while.60 = (s32[]{:T(128)}, f32[2,3,4,128]{3,2,1,0:T(4,128)S(1)}, s32[2]{0:T(128)S(1)}, f32[3,4,2,128]{3,1,0,2:T(4,128)S(1)}, s32[2,4]{1,0:T(2,128)}, /*index=5...) while((s32[]{:T(128)}, f32[2,3,4,128]{3,2,1,0:T(4,128)S(1)}, ...), condition=%wide.region_9.10_spmd.clone, body=%wide.region_4.9_spmd.clone.sunk | while | flops 21691920 | bytes 9811495 | solution.py:140
  45.4 1.9 fusion.196
  48.7 1.2 fusion.198
  50.5 1.3 fusion.199
  56.3 1.9 fusion.196
  59.6 1.2 fusion.198
  61.5 1.3 fusion.199
  63.5 4.6 %collective-permute-start.7 = (f32[3,4,256]{2,1,0:T(4,128)S(1)}, f32[3,4,256]{2,1,0:T(4,128)S(1)}, u32[]{:S(2)}, u32[]{:S(2)}) collective-permute-start(f32[3,4,256]{2,1,0:T(4,128)S(1)} %fusion.122), channel_id=1, source_target_pairs={{2,0},{4,2},{6,4},{8,6},{10,8},{12,10},{14,12},{16,14},{18,16},{20... | collective-permute-start | bytes 36872 | tf_op jit(solution)/shard_map/ppermute | solution.py:29
  68.1 1.2 collective-permute-done.6
  69.5 21.8 %while.61 = (s32[]{:T(128)}, f32[2,3,4,128]{3,2,1,0:T(4,128)S(1)}, s32[2]{0:T(128)S(1)}, f32[3,4,2,128]{3,1,0,2:T(4,128)S(1)}, s32[2,4]{1,0:T(2,128)}, /*index=5...) while((s32[]{:T(128)}, f32[2,3,4,128]{3,2,1,0:T(4,128)S(1)}, ...), condition=%wide.region_15.16_spmd.clone, body=%wide.region_10.15_spmd.clone.sunk | while | flops 21691920 | bytes 9811495 | solution.py:140
  74.0 1.9 fusion.203
  77.3 1.2 fusion.205
  79.2 1.3 fusion.206
  84.9 1.9 fusion.203
  88.2 1.2 fusion.205
  90.1 1.3 fusion.206
  92.1 4.5 %collective-permute-start.9 = (f32[3,4,256]{2,1,0:T(4,128)S(1)}, f32[3,4,256]{2,1,0:T(4,128)S(1)}, u32[]{:S(2)}, u32[]{:S(2)}) collective-permute-start(f32[3,4,256]{2,1,0:T(4,128)S(1)} %fusion.121), channel_id=1, source_target_pairs={{2,0},{4,2},{6,4},{8,6},{10,8},{12,10},{14,12},{16,14},{18,16},{20... | collective-permute-start | bytes 36872 | tf_op jit(solution)/shard_map/ppermute | solution.py:29
  96.6 1.3 collective-permute-done.8
  98.0 21.8 %while.62 = (s32[]{:T(128)}, f32[2,3,4,128]{3,2,1,0:T(4,128)S(1)}, s32[2]{0:T(128)S(1)}, f32[3,4,2,128]{3,1,0,2:T(4,128)S(1)}, s32[2,4]{1,0:T(2,128)}, /*index=5...) while((s32[]{:T(128)}, f32[2,3,4,128]{3,2,1,0:T(4,128)S(1)}, ...), condition=%wide.region_21.22_spmd.clone, body=%wide.region_16.21_spmd.clone.sunk | while | flops 21691920 | bytes 9811495 | solution.py:140
  102.5 1.9 fusion.210
  105.8 1.2 fusion.212
  107.6 1.3 fusion.213
  113.4 1.9 fusion.210
  116.7 1.2 fusion.212
  118.5 1.3 fusion.213
  120.6 4.7 %collective-permute-start.11 = (f32[3,4,256]{2,1,0:T(4,128)S(1)}, f32[3,4,256]{2,1,0:T(4,128)S(1)}, u32[]{:S(2)}, u32[]{:S(2)}) collective-permute-start(f32[3,4,256]{2,1,0:T(4,128)S(1)} %fusion.120), channel_id=1, source_target_pairs={{2,0},{4,2},{6,4},{8,6},{10,8},{12,10},{14,12},{16,14},{18,16},{20... | collective-permute-start | bytes 36872 | tf_op jit(solution)/shard_map/ppermute | solution.py:29
  125.8 1.9 collective-permute-start.14
  128.4 47.7 %while.63 = (s32[]{:T(128)}, f32[2,3,4,128]{3,0,2,1:T(2,128)}, f32[2,3,4,512]{3,2,1,0:T(4,128)}, s32[2]{0:T(128)}, f32[3,4,6,128]{3,1,2,0:T(4,128)S(1)}, /*index...) while((s32[]{:T(128)}, f32[2,3,4,128]{3,0,2,1:T(2,128)}, ...), condition=%wide.region_32.33_spmd.clone, body=%wide.region_22.32_spmd.clone.sunk | while | flops 64432148 | bytes 27084660 | solution.py:161
  128.4 1.3 dynamic_slice.237
  134.4 3.9 %fusion.218 = (f32[4,128,512]{2,1,0:T(8,128)S(1)}, f32[4,128,512]{2,1,0:T(8,128)S(1)}, f32[4,128,512]{2,1,0:T(8,128)S(1)}, f32[4,128,512]{2,1,0:T(8,128)}) fusion(f32[3]{0:T(128)} %get-tuple-element.1644, f32[3]{0:T(128)} %get-tuple-element.1645, f32[3,4,512]{2,1,0:T(4,128)S(1)} %get-tuple-element.1380, ...), kind=kLoop, calls=%fused_computation.179.clone.1 | loop fusion | flops 9961472 | bytes 4261912 | tf_op jit(solution)/shard_map/while/body/eval_jaxpr/jvp()/reduce_sum | solution.py:42
  139.8 4.2 %fusion.220 = (f32[4,128,512]{2,1,0:T(8,128)S(1)}, f32[4,128,512]{2,1,0:T(8,128)S(1)}, f32[4,128,512]{2,1,0:T(8,128)S(1)}) fusion(f32[4,128,512]{2,1,0:T(8,128)S(1)} %get-tuple-element.1384, f32[128,512]{1,0:T(8,128)S(1)} %multiply_sqrt_fusion.14, f32[128,512]{1,0:T(8,128)S(1)} %compare_select_fusion.19, f32[4,128,512]{2,1,0:T(8,128)S(1)} %get-tuple-element.1387, ...), kind=kLoop, calls=%fused_computation.239.clone.1 | loop fusion | flops 20185088 | bytes 7864320 | tf_op jit(solution)/shard_map/while/body/eval_jaxpr/jvp()/mul | solution.py:62
  143.9 0.7 multiply_bitcast_fusion.4
  144.7 2.4 %fusion.221 = (f32[3,4,512]{2,1,0:T(4,128)S(1)}, f32[3,4,128]{2,1,0:T(4,128)S(1)}, f32[4,128,512]{2,1,0:T(8,128)S(1)}) fusion(f32[3]{0:T(128)S(1)} %copy-done.6, f32[4,128,512]{2,1,0:T(8,128)S(1)} %get-tuple-element.1390, f32[4,128,512]{2,1,0:T(8,128)S(1)} %get-tuple-element.1391, f32[4,128,512]{2,1,0:T(8,128)S(1)} %get-tuple-element.1392, ...), kind=kLoop, calls=%fused_computation.186.clone.1 | loop fusion | flops 12313088 | bytes 4292632 | tf_op jit(solution)/shard_map/while/body/eval_jaxpr/transpose(jvp())/reduce_sum | solution.py:40
  147.7 1.9 divide_multiply_fusion.2
  149.6 1.9 fusion.222
  152.3 1.3 dynamic_slice.237
  158.3 3.9 %fusion.218 = (f32[4,128,512]{2,1,0:T(8,128)S(1)}, f32[4,128,512]{2,1,0:T(8,128)S(1)}, f32[4,128,512]{2,1,0:T(8,128)S(1)}, f32[4,128,512]{2,1,0:T(8,128)}) fusion(f32[3]{0:T(128)} %get-tuple-element.1644, f32[3]{0:T(128)} %get-tuple-element.1645, f32[3,4,512]{2,1,0:T(4,128)S(1)} %get-tuple-element.1380, ...), kind=kLoop, calls=%fused_computation.179.clone.1 | loop fusion | flops 9961472 | bytes 4261912 | tf_op jit(solution)/shard_map/while/body/eval_jaxpr/jvp()/reduce_sum | solution.py:42
  163.6 4.2 %fusion.220 = (f32[4,128,512]{2,1,0:T(8,128)S(1)}, f32[4,128,512]{2,1,0:T(8,128)S(1)}, f32[4,128,512]{2,1,0:T(8,128)S(1)}) fusion(f32[4,128,512]{2,1,0:T(8,128)S(1)} %get-tuple-element.1384, f32[128,512]{1,0:T(8,128)S(1)} %multiply_sqrt_fusion.14, f32[128,512]{1,0:T(8,128)S(1)} %compare_select_fusion.19, f32[4,128,512]{2,1,0:T(8,128)S(1)} %get-tuple-element.1387, ...), kind=kLoop, calls=%fused_computation.239.clone.1 | loop fusion | flops 20185088 | bytes 7864320 | tf_op jit(solution)/shard_map/while/body/eval_jaxpr/jvp()/mul | solution.py:62
  167.8 0.7 multiply_bitcast_fusion.4
  168.5 2.4 %fusion.221 = (f32[3,4,512]{2,1,0:T(4,128)S(1)}, f32[3,4,128]{2,1,0:T(4,128)S(1)}, f32[4,128,512]{2,1,0:T(8,128)S(1)}) fusion(f32[3]{0:T(128)S(1)} %copy-done.6, f32[4,128,512]{2,1,0:T(8,128)S(1)} %get-tuple-element.1390, f32[4,128,512]{2,1,0:T(8,128)S(1)} %get-tuple-element.1391, f32[4,128,512]{2,1,0:T(8,128)S(1)} %get-tuple-element.1392, ...), kind=kLoop, calls=%fused_computation.186.clone.1 | loop fusion | flops 12313088 | bytes 4292632 | tf_op jit(solution)/shard_map/while/body/eval_jaxpr/transpose(jvp())/reduce_sum | solution.py:40
  171.5 1.9 divide_multiply_fusion.2
  173.4 1.9 fusion.222
  176.1 0.8 reshape.866
  176.9 1.0 convolution_bitcast_fusion
  177.9 0.7 fusion.130
  178.7 3.2 %collective-permute-start.12 = (f32[3,4,256]{2,1,0:T(4,128)S(1)}, f32[3,4,256]{2,1,0:T(4,128)S(1)}, u32[]{:S(2)}, u32[]{:S(2)}) collective-permute-start(f32[3,4,256]{2,1,0:T(4,128)S(1)} %reshape.868), channel_id=1, source_target_pairs={{0,30},{2,0},{4,2},{6,4},{8,6},{10,8},{12,10},{14,12},{16,14},{18,... | collective-permute-start | bytes 36872 | tf_op jit(solution)/shard_map/ppermute | solution.py:36
  182.0 1.3 fusion.119
  183.3 38.9 %psum.7 = f32[]{:T(128)} all-reduce(f32[]{:T(128)} %fusion.119), channel_id=1, replica_groups=mesh['space'=16,'bead'=2] {'space','bead'}, use_global_device_ids=true, to_apply=%region_34.35 | all-reduce | flops 1 | bytes 8 | tf_op jit(solution)/shard_map/psum | solution.py:174
  223.0 1.5 multiply_add_fusion
  (291 shorter events, 50.0 us)
Async XLA Ops:
  2.2 12.7 %collective-permute-start = (f32[3,4,256]{2,1,0:T(4,128)S(1)}, f32[3,4,256]{2,1,0:T(4,128)S(1)}, u32[]{:S(2)}, u32[]{:S(2)}) collective-permute-start(f32[3,4,256]{2,1,0:T(4,128)S(1)} %broadcast_add_fusion), channel_id=1, source_target_pairs={{0,2},{2,4},{4,6},{6,8},{8,10},{10,12},{12,14},{14,16},{16,18},{18... | collective-permute-start | bytes 36872 | tf_op jit(solution)/shard_map/ppermute | solution.py:28
  2.7 12.2 %collective-permute-start.1 = (f32[3,4,256]{2,1,0:T(4,128)S(1)}, f32[3,4,256]{2,1,0:T(4,128)S(1)}, u32[]{:S(2)}, u32[]{:S(2)}) collective-permute-start(f32[3,4,256]{2,1,0:T(4,128)S(1)} %broadcast_add_fusion), channel_id=1, source_target_pairs={{2,0},{4,2},{6,4},{8,6},{10,8},{12,10},{14,12},{16,14},{18,16},{20... | collective-permute-start | bytes 36872 | tf_op jit(solution)/shard_map/ppermute | solution.py:29
  9.0 5.8 %collective-permute-start.2 = (f32[3,1,256]{2,1,0:T(1,128)S(1)}, f32[3,1,256]{2,1,0:T(1,128)S(1)}, u32[]{:S(2)}, u32[]{:S(2)}) collective-permute-start(f32[3,1,256]{2,1,0:T(1,128)S(1)} %broadcast_in_dim.161), channel_id=1, source_target_pairs={{0,2},{2,4},{4,6},{6,8},{8,10},{10,12},{12,14},{14,16},{16,18},{18... | collective-permute-start | bytes 9224 | tf_op jit(solution)/shard_map/ppermute | solution.py:28
  9.1 5.7 %collective-permute-start.3 = (f32[3,1,256]{2,1,0:T(1,128)S(1)}, f32[3,1,256]{2,1,0:T(1,128)S(1)}, u32[]{:S(2)}, u32[]{:S(2)}) collective-permute-start(f32[3,1,256]{2,1,0:T(1,128)S(1)} %broadcast_in_dim.161), channel_id=1, source_target_pairs={{2,0},{4,2},{6,4},{8,6},{10,8},{12,10},{14,12},{16,14},{18,16},{20... | collective-permute-start | bytes 9224 | tf_op jit(solution)/shard_map/ppermute | solution.py:29
  15.0 6.1 %copy-start.14 = (f32[2,128]{1,0:T(2,128)S(1)}, f32[2,128]{1,0:T(2,128)}, u32[]{:S(2)}) copy-start(f32[2,128]{1,0:T(2,128)} %get-tuple-element.1440) | copy-start | bytes 3076 | tf_op jit(solution)/shard_map/while
  22.4 0.9 copy-start.2
  22.4 0.9 copy-start.7
  24.7 6.1 %copy-start.14 = (f32[2,128]{1,0:T(2,128)S(1)}, f32[2,128]{1,0:T(2,128)}, u32[]{:S(2)}) copy-start(f32[2,128]{1,0:T(2,128)} %get-tuple-element.1440) | copy-start | bytes 3076 | tf_op jit(solution)/shard_map/while
  32.1 0.9 copy-start.2
  32.1 0.9 copy-start.7
  35.0 5.8 %collective-permute-start.4 = (f32[3,4,256]{2,1,0:T(4,128)S(1)}, f32[3,4,256]{2,1,0:T(4,128)S(1)}, u32[]{:S(2)}, u32[]{:S(2)}) collective-permute-start(f32[3,4,256]{2,1,0:T(4,128)S(1)} %bitcast_multiply_fusion), channel_id=1, source_target_pairs={{0,2},{2,4},{4,6},{6,8},{8,10},{10,12},{12,14},{14,16},{16,18},{18... | collective-permute-start | bytes 36872 | tf_op jit(solution)/shard_map/ppermute | solution.py:28
  35.0 5.8 %collective-permute-start.5 = (f32[3,4,256]{2,1,0:T(4,128)S(1)}, f32[3,4,256]{2,1,0:T(4,128)S(1)}, u32[]{:S(2)}, u32[]{:S(2)}) collective-permute-start(f32[3,4,256]{2,1,0:T(4,128)S(1)} %bitcast_multiply_fusion), channel_id=1, source_target_pairs={{2,0},{4,2},{6,4},{8,6},{10,8},{12,10},{14,12},{16,14},{18,16},{20... | collective-permute-start | bytes 36872 | tf_op jit(solution)/shard_map/ppermute | solution.py:29
  45.3 2.5 %copy-start.15 = (f32[2,128]{1,0:T(2,128)S(1)}, f32[2,128]{1,0:T(2,128)}, u32[]{:S(2)}) copy-start(f32[2,128]{1,0:T(2,128)} %get-tuple-element.1488) | copy-start | bytes 3076 | tf_op jit(solution)/shard_map/while
  49.9 0.7 copy-start.3
  49.9 0.7 copy-start.8
  56.3 2.5 %copy-start.15 = (f32[2,128]{1,0:T(2,128)S(1)}, f32[2,128]{1,0:T(2,128)}, u32[]{:S(2)}) copy-start(f32[2,128]{1,0:T(2,128)} %get-tuple-element.1488) | copy-start | bytes 3076 | tf_op jit(solution)/shard_map/while
  60.8 0.7 copy-start.3
  60.8 0.7 copy-start.8
  63.5 5.8 %collective-permute-start.6 = (f32[3,4,256]{2,1,0:T(4,128)S(1)}, f32[3,4,256]{2,1,0:T(4,128)S(1)}, u32[]{:S(2)}, u32[]{:S(2)}) collective-permute-start(f32[3,4,256]{2,1,0:T(4,128)S(1)} %fusion.122), channel_id=1, source_target_pairs={{0,2},{2,4},{4,6},{6,8},{8,10},{10,12},{12,14},{14,16},{16,18},{18... | collective-permute-start | bytes 36872 | tf_op jit(solution)/shard_map/ppermute | solution.py:28
  63.5 6.1 %collective-permute-start.7 = (f32[3,4,256]{2,1,0:T(4,128)S(1)}, f32[3,4,256]{2,1,0:T(4,128)S(1)}, u32[]{:S(2)}, u32[]{:S(2)}) collective-permute-start(f32[3,4,256]{2,1,0:T(4,128)S(1)} %fusion.122), channel_id=1, source_target_pairs={{2,0},{4,2},{6,4},{8,6},{10,8},{12,10},{14,12},{16,14},{18,16},{20... | collective-permute-start | bytes 36872 | tf_op jit(solution)/shard_map/ppermute | solution.py:29
  74.0 2.5 %copy-start.16 = (f32[2,128]{1,0:T(2,128)S(1)}, f32[2,128]{1,0:T(2,128)}, u32[]{:S(2)}) copy-start(f32[2,128]{1,0:T(2,128)} %get-tuple-element.1536) | copy-start | bytes 3076 | tf_op jit(solution)/shard_map/while
  78.5 0.7 copy-start.4
  78.5 0.7 copy-start.9
  84.9 2.5 %copy-start.16 = (f32[2,128]{1,0:T(2,128)S(1)}, f32[2,128]{1,0:T(2,128)}, u32[]{:S(2)}) copy-start(f32[2,128]{1,0:T(2,128)} %get-tuple-element.1536) | copy-start | bytes 3076 | tf_op jit(solution)/shard_map/while
  89.4 0.7 copy-start.4
  89.4 0.7 copy-start.9
  92.1 5.8 %collective-permute-start.8 = (f32[3,4,256]{2,1,0:T(4,128)S(1)}, f32[3,4,256]{2,1,0:T(4,128)S(1)}, u32[]{:S(2)}, u32[]{:S(2)}) collective-permute-start(f32[3,4,256]{2,1,0:T(4,128)S(1)} %fusion.121), channel_id=1, source_target_pairs={{0,2},{2,4},{4,6},{6,8},{8,10},{10,12},{12,14},{14,16},{16,18},{18... | collective-permute-start | bytes 36872 | tf_op jit(solution)/shard_map/ppermute | solution.py:28
  92.1 5.9 %collective-permute-start.9 = (f32[3,4,256]{2,1,0:T(4,128)S(1)}, f32[3,4,256]{2,1,0:T(4,128)S(1)}, u32[]{:S(2)}, u32[]{:S(2)}) collective-permute-start(f32[3,4,256]{2,1,0:T(4,128)S(1)} %fusion.121), channel_id=1, source_target_pairs={{2,0},{4,2},{6,4},{8,6},{10,8},{12,10},{14,12},{16,14},{18,16},{20... | collective-permute-start | bytes 36872 | tf_op jit(solution)/shard_map/ppermute | solution.py:29
  98.0 27.3 %copy-start.19 = (f32[3,4,256]{2,1,0:T(4,128)S(1)}, f32[3,4,256]{2,1,0:T(4,128)}, u32[]{:S(2)}) copy-start(f32[3,4,256]{2,1,0:T(4,128)} %param.20) | copy-start | bytes 36868
  102.4 2.5 %copy-start.17 = (f32[2,128]{1,0:T(2,128)S(1)}, f32[2,128]{1,0:T(2,128)}, u32[]{:S(2)}) copy-start(f32[2,128]{1,0:T(2,128)} %get-tuple-element.1584) | copy-start | bytes 3076 | tf_op jit(solution)/shard_map/while
  106.9 0.7 copy-start.5
  107.0 0.7 copy-start.10
  113.4 2.5 %copy-start.17 = (f32[2,128]{1,0:T(2,128)S(1)}, f32[2,128]{1,0:T(2,128)}, u32[]{:S(2)}) copy-start(f32[2,128]{1,0:T(2,128)} %get-tuple-element.1584) | copy-start | bytes 3076 | tf_op jit(solution)/shard_map/while
  117.9 0.7 copy-start.5
  117.9 0.7 copy-start.10
  120.5 7.9 %copy-start.22 = (f32[3,4,256]{2,1,0:T(4,128)}, f32[3,4,256]{2,1,0:T(4,128)S(1)}, u32[]{:S(2)}) copy-start(f32[3,4,256]{2,1,0:T(4,128)S(1)} %fusion.120) | copy-start | bytes 36868
  120.5 7.3 %collective-permute-start.10 = (f32[3,4,256]{2,1,0:T(4,128)S(1)}, f32[3,4,256]{2,1,0:T(4,128)S(1)}, u32[]{:S(2)}, u32[]{:S(2)}) collective-permute-start(f32[3,4,256]{2,1,0:T(4,128)S(1)} %fusion.120), channel_id=1, source_target_pairs={{0,2},{2,4},{4,6},{6,8},{8,10},{10,12},{12,14},{14,16},{16,18},{18... | collective-permute-start | bytes 36872 | tf_op jit(solution)/shard_map/ppermute | solution.py:28
  120.6 7.3 %collective-permute-start.11 = (f32[3,4,256]{2,1,0:T(4,128)S(1)}, f32[3,4,256]{2,1,0:T(4,128)S(1)}, u32[]{:S(2)}, u32[]{:S(2)}) collective-permute-start(f32[3,4,256]{2,1,0:T(4,128)S(1)} %fusion.120), channel_id=1, source_target_pairs={{2,0},{4,2},{6,4},{8,6},{10,8},{12,10},{14,12},{16,14},{18,16},{20... | collective-permute-start | bytes 36872 | tf_op jit(solution)/shard_map/ppermute | solution.py:29
  125.8 97.1 %collective-permute-start.14 = (f32[3,1,256]{2,1,0:T(1,128)}, f32[3,1,256]{2,1,0:T(1,128)}, u32[]{:S(2)}, u32[]{:S(2)}) collective-permute-start(f32[3,1,256]{2,1,0:T(1,128)} %get-tuple-element.954), channel_id=1, source_target_pairs={{0,1},{1,0},{2,3},{3,2},{4,5},{5,4},{6,7},{7,6},{8,9},{9,8},{10,11... | collective-permute-start | bytes 9224 | tf_op jit(solution)/shard_map/ppermute | solution.py:28
  127.8 95.2 %collective-permute-start.15 = (f32[3,1,256]{2,1,0:T(1,128)}, f32[3,1,256]{2,1,0:T(1,128)}, u32[]{:S(2)}, u32[]{:S(2)}) collective-permute-start(f32[3,1,256]{2,1,0:T(1,128)} %get-tuple-element.955), channel_id=1, source_target_pairs={{1,0},{0,1},{3,2},{2,3},{5,4},{4,5},{7,6},{6,7},{9,8},{8,9},{11,10... | collective-permute-start | bytes 9224 | tf_op jit(solution)/shard_map/ppermute | solution.py:29
  128.4 6.0 %copy-start.12 = (f32[3,4,6,128]{3,1,2,0:T(4,128)}, f32[3,4,6,128]{3,1,2,0:T(4,128)S(1)}, u32[]{:S(2)}) copy-start(f32[3,4,6,128]{3,1,2,0:T(4,128)S(1)} %get-tuple-element.1634) | copy-start | bytes 110596 | tf_op jit(solution)/shard_map/while
  134.4 4.5 %copy-start.18 = (f32[2,128]{1,0:T(2,128)S(1)}, f32[2,128]{1,0:T(2,128)}, u32[]{:S(2)}) copy-start(f32[2,128]{1,0:T(2,128)} %get-tuple-element.1640) | copy-start | bytes 3076 | tf_op jit(solution)/shard_map/while
  139.7 4.2 %copy-start = (f32[128,512]{1,0:T(8,128)}, f32[128,512]{1,0:T(8,128)S(1)}, u32[]{:S(2)}) copy-start(f32[128,512]{1,0:T(8,128)S(1)} %multiply_sqrt_fusion.14) | copy-start | bytes 786436 | tf_op jit(solution)/shard_map/while
  139.7 4.9 %copy-start.6 = (f32[3]{0:T(128)S(1)}, f32[3]{0:T(128)}, u32[]{:S(2)}) copy-start(f32[3]{0:T(128)} %get-tuple-element.1644) | copy-start | bytes 40 | tf_op jit(solution)/shard_map/while
  139.7 4.9 %copy-start.11 = (f32[3]{0:T(128)S(1)}, f32[3]{0:T(128)}, u32[]{:S(2)}) copy-start(f32[3]{0:T(128)} %get-tuple-element.1645) | copy-start | bytes 40 | tf_op jit(solution)/shard_map/while
  144.7 3.0 %copy-start.1 = (f32[128,512]{1,0:T(8,128)S(1)}, f32[128,512]{1,0:T(8,128)}, u32[]{:S(2)}) copy-start(f32[128,512]{1,0:T(8,128)} %copy-done) | copy-start | bytes 786436 | tf_op jit(solution)/shard_map/while
  149.6 2.0 copy-start.20
  149.6 2.0 copy-start.23
  149.6 2.7 %copy-start.13 = (f32[3,4,6,128]{3,1,2,0:T(4,128)S(1)}, f32[3,4,6,128]{3,1,2,0:T(4,128)}, u32[]{:S(2)}) copy-start(f32[3,4,6,128]{3,1,2,0:T(4,128)} %copy-done.12) | copy-start | bytes 110596 | tf_op jit(solution)/shard_map/while
  151.6 0.6 copy-start.21
  151.7 0.6 copy-start.24
  152.3 6.0 %copy-start.12 = (f32[3,4,6,128]{3,1,2,0:T(4,128)}, f32[3,4,6,128]{3,1,2,0:T(4,128)S(1)}, u32[]{:S(2)}) copy-start(f32[3,4,6,128]{3,1,2,0:T(4,128)S(1)} %get-tuple-element.1634) | copy-start | bytes 110596 | tf_op jit(solution)/shard_map/while
  158.2 4.5 %copy-start.18 = (f32[2,128]{1,0:T(2,128)S(1)}, f32[2,128]{1,0:T(2,128)}, u32[]{:S(2)}) copy-start(f32[2,128]{1,0:T(2,128)} %get-tuple-element.1640) | copy-start | bytes 3076 | tf_op jit(solution)/shard_map/while
  163.6 4.2 %copy-start = (f32[128,512]{1,0:T(8,128)}, f32[128,512]{1,0:T(8,128)S(1)}, u32[]{:S(2)}) copy-start(f32[128,512]{1,0:T(8,128)S(1)} %multiply_sqrt_fusion.14) | copy-start | bytes 786436 | tf_op jit(solution)/shard_map/while
  163.6 4.9 %copy-start.6 = (f32[3]{0:T(128)S(1)}, f32[3]{0:T(128)}, u32[]{:S(2)}) copy-start(f32[3]{0:T(128)} %get-tuple-element.1644) | copy-start | bytes 40 | tf_op jit(solution)/shard_map/while
  163.6 4.9 %copy-start.11 = (f32[3]{0:T(128)S(1)}, f32[3]{0:T(128)}, u32[]{:S(2)}) copy-start(f32[3]{0:T(128)} %get-tuple-element.1645) | copy-start | bytes 40 | tf_op jit(solution)/shard_map/while
  168.5 3.0 %copy-start.1 = (f32[128,512]{1,0:T(8,128)S(1)}, f32[128,512]{1,0:T(8,128)}, u32[]{:S(2)}) copy-start(f32[128,512]{1,0:T(8,128)} %copy-done) | copy-start | bytes 786436 | tf_op jit(solution)/shard_map/while
  173.4 2.0 copy-start.20
  173.4 2.0 copy-start.23
  173.4 2.7 %copy-start.13 = (f32[3,4,6,128]{3,1,2,0:T(4,128)S(1)}, f32[3,4,6,128]{3,1,2,0:T(4,128)}, u32[]{:S(2)}) copy-start(f32[3,4,6,128]{3,1,2,0:T(4,128)} %copy-done.12) | copy-start | bytes 110596 | tf_op jit(solution)/shard_map/while
  175.4 0.6 copy-start.21
  175.5 0.6 copy-start.24
  178.7 44.3 %collective-permute-start.12 = (f32[3,4,256]{2,1,0:T(4,128)S(1)}, f32[3,4,256]{2,1,0:T(4,128)S(1)}, u32[]{:S(2)}, u32[]{:S(2)}) collective-permute-start(f32[3,4,256]{2,1,0:T(4,128)S(1)} %reshape.868), channel_id=1, source_target_pairs={{0,30},{2,0},{4,2},{6,4},{8,6},{10,8},{12,10},{14,12},{16,14},{18,... | collective-permute-start | bytes 36872 | tf_op jit(solution)/shard_map/ppermute | solution.py:36
  181.9 41.1 %collective-permute-start.13 = (f32[3,4,256]{2,1,0:T(4,128)S(1)}, f32[3,4,256]{2,1,0:T(4,128)S(1)}, u32[]{:S(2)}, u32[]{:S(2)}) collective-permute-start(f32[3,4,256]{2,1,0:T(4,128)S(1)} %reshape.869), channel_id=1, source_target_pairs={{0,2},{2,4},{4,6},{6,8},{8,10},{10,12},{12,14},{14,16},{16,18},{18... | collective-permute-start | bytes 36872 | tf_op jit(solution)/shard_map/ppermute | solution.py:36
where the time goes:
time: 226 us; the launch traced here: 224 us
  other arithmetic  85.1 us (38%)
  blocking collectives  38.9 us (17%)
  local copies, waits for them, and re-layouts  37.1 us (16%)
  starting transfers between devices  33.5 us (15%)
  loops' own time  22.4 us (10%)
  waiting for transfers between devices  4.82 us (2%)
    psum x1, blocking collectives, per_device(): lax.psum(jnp.sum(masses[None, None, :] * velocities * velocities), ('spac...  38.9 us
    ppermute x7, starting transfers between devices, extended(): after = lax.ppermute(first, axis, down)  27.7 us
    reduce_sum x10, other arithmetic, geometry(): square = jnp.sum(delta * delta, axis=0) + 1.0  22.7 us
    another operation x3, loops' own time, per_device(): mu = polar * (field0 + spread(lax.map(one, order)))  12.3 us
    reduce_sum x4, other arithmetic, geometry(): delta = xi[:, :, :, None] - xj[:, :, None, :]  8.7 us
    mul x2, other arithmetic, mutual(): inv_five * along  8.35 us
    reduce_sum x6, other arithmetic, mutual(): jnp.sum(delta * (inv_five * along)[None], axis=-1)  7.68 us
    dynamic_slice x10, local copies, waits for them, and re-layouts, per_device(): field0 = spread(lax.map(perm_block, order))  7.25 us
  transfers between devices with their start and end apart: 16, of which 6 were waited for; matrix products, arithmetic and copies ran while one was open for 21% of the time, Pallas kernels for 0%

commit v1 on v0

v1 whole, which is shorter than its diff:
```python
import functools

import jax
import jax.numpy as jnp
from jax import lax
from jax.experimental import pallas as pl
from jax.experimental.pallas import tpu as pltpu
from jax.sharding import PartitionSpec as P

BLOCK = 128
NT = 4
ITERS = 3
GROUPS = 2
R_GEO = 16
R_MUT = 32
R_FRC = 16

slab_width = 9.0
box_side = 24.0
cut_square = 64.0
thole_coef = 0.39
bond_coef = 4.0
time_step = 0.05
target_temp = 8.0
coupling = 0.5


def spread(col, k):
    return jnp.broadcast_to(col[:, k : k + 1], (col.shape[0], BLOCK))


def fold(value):
    total = value[0:8]
    for i in range(1, value.shape[0] // 8):
        total = total + value[8 * i : 8 * i + 8]
    return total


def kernel(
    ns,
    nbd,
    cen_ref,
    off_ref,
    vel_ref,
    chg_ref,
    pol_ref,
    mass_ref,
    grp_ref,
    tiles_ref,
    mu_out,
    force_out,
    vel_out,
    off_out,
    p_own,
    p_halo,
    col_p,
    geo,
    f0,
    mu_own,
    mu_halo,
    col_m,
    col_r,
    r_own,
    r_send,
    r_recv,
    f_own,
    ob,
    k_own,
    k_recv,
    p_ss,
    p_rs,
    m_ss,
    m_rs,
    r_ss,
    r_rs,
    o_ss,
    o_rs,
    k_ss,
    k_rs,
):
    beads = off_ref.shape[1]
    nblk = off_ref.shape[2] // BLOCK
    nb = beads // GROUPS
    me = lax.axis_index("space")
    mb = lax.axis_index("bead")
    right, left = lax.rem(me + 1, ns), lax.rem(me + ns - 1, ns)
    above, below = lax.rem(mb + 1, nbd), lax.rem(mb + nbd - 1, nbd)
    partners = []
    step = 1
    while step < ns:
        partners.append({"space": me + step - 2 * step * ((me // step) % 2)})
        step *= 2
    step = 1
    while step < nbd:
        partners.append({"bead": mb + step - 2 * step * ((mb // step) % 2)})
        step *= 2

    barrier = pltpu.get_barrier_semaphore()
    everyone = [{"space": right}, {"space": left}, {"bead": above}, {"bead": below}] + partners
    for who in everyone:
        pl.semaphore_signal(barrier, inc=1, device_id=who, device_id_type=pl.DeviceIdType.MESH)

    pending = []

    def send(src, dst, ss, rs, who):
        copy = pltpu.make_async_remote_copy(
            src_ref=src,
            dst_ref=dst,
            send_sem=ss,
            recv_sem=rs,
            device_id=who,
            device_id_type=pl.DeviceIdType.MESH,
        )
        copy.start()
        pending.append(copy)
        return copy

    for b in range(nblk):
        cut = slice(b * BLOCK, (b + 1) * BLOCK)
        p_own[b, 0:beads, :] = cen_ref[0:1, cut] * slab_width + off_ref[0, :, cut]
        for c in (1, 2):
            p_own[b, c * beads : (c + 1) * beads, :] = cen_ref[c : c + 1, cut] + off_ref[
                c, :, cut
            ] * (1.0 / box_side)
        base = 3 * beads
        p_own[b, base : base + 1, :] = chg_ref[0:1, cut]
        p_own[b, base + 1 : base + 2, :] = lax.rsqrt(pol_ref[0:1, cut])
        p_own[b, base + 2 : base + 3, :] = grp_ref[0:1, cut].astype(jnp.float32)
        p_own[b, base + 3 : base + 4, :] = pol_ref[0:1, cut]
    heat = jnp.zeros((beads, off_ref.shape[2]), jnp.float32)
    for c in range(3):
        heat = heat + vel_ref[c] * vel_ref[c]
    heat = heat * mass_ref[0:1, :]
    tally = heat[:, 0:BLOCK]
    for b in range(1, nblk):
        tally = tally + heat[:, b * BLOCK : (b + 1) * BLOCK]
    k_own[0] = jnp.zeros((8, BLOCK), jnp.float32)
    k_own[0, 0:beads, :] = tally
    for g in range(GROUPS):
        for s in range(ITERS + 1):
            mu_own[g, s] = jnp.zeros(mu_own.shape[2:], jnp.float32)

    pl.semaphore_wait(barrier, len(everyone))

    to_right = send(p_own, p_halo.at[0], p_ss.at[0], p_rs.at[0], {"space": right})
    to_left = send(p_own, p_halo.at[1], p_ss.at[1], p_rs.at[1], {"space": left})
    bead_up = send(off_ref, ob.at[0], o_ss.at[0], o_rs.at[0], {"bead": above})
    bead_down = send(off_ref, ob.at[1], o_ss.at[1], o_rs.at[1], {"bead": below})

    heat_state = {"stage": 0, "copy": None}

    def heat_send():
        s = heat_state["stage"]
        heat_state["copy"] = send(
            k_own.at[s], k_recv.at[s], k_ss.at[s], k_rs.at[s], partners[s]
        )

    def heat_step():
        s = heat_state["stage"]
        if s >= len(partners):
            return
        heat_state["copy"].wait_recv()
        k_own[s + 1] = k_own[s] + k_recv[s]
        heat_state["stage"] = s + 1
        if s + 1 < len(partners):
            heat_send()

    heat_send()

    for b in range(nblk):
        col_p[nblk + b] = p_own[b].T
    for d, copy in ((0, to_right), (1, to_left)):
        copy.wait_recv()
        move = -slab_width if d == 0 else slab_width
        row = lax.broadcasted_iota(jnp.int32, p_own.shape[1:], 0)
        for b in range(nblk):
            col_p[2 * d * nblk + b] = jnp.where(
                row < beads, p_halo[d, b] + move, p_halo[d, b]
            ).T
    heat_step()

    def geometry(g):
        chunks = BLOCK // R_GEO

        def block(b, none):
            own = p_own[b]
            full = (R_GEO, BLOCK)
            ki = jnp.broadcast_to(own[3 * beads + 1 : 3 * beads + 2] * thole_coef, full)
            gi = jnp.broadcast_to(own[3 * beads + 2 : 3 * beads + 3], full)
            xi = [
                [
                    jnp.broadcast_to(own[c * beads + g * nb + k : c * beads + g * nb + k + 1], full)
                    for c in range(3)
                ]
                for k in range(nb)
            ]

            def chunk(m, accs):
                e = tiles_ref[b, m // chunks]
                start = pl.multiple_of((m % chunks) * R_GEO, R_GEO)
                col = col_p[e, pl.ds(start, R_GEO), :]
                qj = spread(col, 3 * beads)
                kk = ki * spread(col, 3 * beads + 1)
                mask = jnp.where(gi == spread(col, 3 * beads + 2), 0.0, 1.0)
                rows = pl.ds(pl.multiple_of(b * (NT * BLOCK) + m * R_GEO, R_GEO), R_GEO)
                out = []
                for k in range(nb):
                    bead = g * nb + k
                    dx = xi[k][0] - spread(col, bead)
                    dy = xi[k][1] - spread(col, beads + bead)
                    dy = (dy - jnp.floor(dy + 0.5)) * box_side
                    dz = xi[k][2] - spread(col, 2 * beads + bead)
                    dz = (dz - jnp.floor(dz + 0.5)) * box_side
                    s = dx * dx + dy * dy + dz * dz + 1.0
                    r = lax.rsqrt(s)
                    r2 = r * r
                    u = kk * (s * s * r)
                    fade = jnp.exp(-u)
                    ue = u * fade
                    l3 = 1.0 - fade
                    l5 = l3 - ue
                    t = jnp.maximum(1.0 - s * (1.0 / cut_square), 0.0)
                    tm = t * mask
                    w = tm * t
                    r3 = r2 * r
                    wr3 = w * r3
                    b3 = wr3 * l3
                    wr5 = wr3 * r2 * 3.0
                    b5 = wr5 * l5
                    slope = tm * r3 * (-2.0 / cut_square)
                    d3 = 2.0 * slope * l3 + 3.0 * (wr3 * r2) * (ue - l3)
                    d5 = r2 * (3.0 * slope * l5 + wr5 * (1.5 * u * ue - 2.5 * l5))
                    geo[0, bead, rows, :] = dx
                    geo[1, bead, rows, :] = dy
                    geo[2, bead, rows, :] = dz
                    geo[3, bead, rows, :] = b3
                    geo[4, bead, rows, :] = b5
                    geo[5, bead, rows, :] = d3
                    geo[6, bead, rows, :] = d5
                    qb = qj * b3
                    out += [
                        accs[3 * k] + fold(qb * dx),
                        accs[3 * k + 1] + fold(qb * dy),
                        accs[3 * k + 2] + fold(qb * dz),
                    ]
                return tuple(out)

            zero = jnp.zeros((8, BLOCK), jnp.float32)
            accs = lax.fori_loop(0, NT * chunks, chunk, (zero,) * (3 * nb))
            pol = own[3 * beads + 3 : 3 * beads + 4]
            for k in range(nb):
                for c in range(3):
                    field = jnp.sum(accs[3 * k + c], axis=0, keepdims=True)
                    f0[g, b, c * nb + k : c * nb + k + 1, :] = field
                    mu_own[g, 0, b, c * nb + k : c * nb + k + 1, :] = pol * field
            return none

        lax.fori_loop(0, nblk, block, 0)

    def mu_send(g, s):
        n = 2 * (g * (ITERS + 1) + s)
        return (
            send(mu_own.at[g, s], mu_halo.at[g, s, 0], m_ss.at[n], m_rs.at[n], {"space": right}),
            send(
                mu_own.at[g, s], mu_halo.at[g, s, 1], m_ss.at[n + 1], m_rs.at[n + 1], {"space": left}
            ),
        )

    def mu_columns(g, s, copies):
        for b in range(nblk):
            col_m[g, nblk + b] = mu_own[g, s, b].T
        for d in range(2):
            copies[d].wait_recv()
            for b in range(nblk):
                col_m[g, 2 * d * nblk + b] = mu_halo[g, s, d, b].T

    def mutual(g, s):
        chunks = BLOCK // R_MUT

        def block(b, none):
            def chunk(m, accs):
                e = tiles_ref[b, m // chunks]
                start = pl.multiple_of((m % chunks) * R_MUT, R_MUT)
                col = col_m[g, e, pl.ds(start, R_MUT), :]
                rows = pl.ds(pl.multiple_of(b * (NT * BLOCK) + m * R_MUT, R_MUT), R_MUT)
                out = []
                for k in range(nb):
                    bead = g * nb + k
                    mx, my, mz = (spread(col, k), spread(col, nb + k), spread(col, 2 * nb + k))
                    dx, dy, dz = (geo[0, bead, rows, :], geo[1, bead, rows, :], geo[2, bead, rows, :])
                    b3 = geo[3, bead, rows, :]
                    along = geo[4, bead, rows, :] * (dx * mx + dy * my + dz * mz)
                    out += [
                        accs[3 * k] + fold(along * dx - b3 * mx),
                        accs[3 * k + 1] + fold(along * dy - b3 * my),
                        accs[3 * k + 2] + fold(along * dz - b3 * mz),
                    ]
                return tuple(out)

            zero = jnp.zeros((8, BLOCK), jnp.float32)
            accs = lax.fori_loop(0, NT * chunks, chunk, (zero,) * (3 * nb))
            pol = p_own[b, 3 * beads + 3 : 3 * beads + 4, :]
            for k in range(nb):
                for c in range(3):
                    row = slice(c * nb + k, c * nb + k + 1)
                    field = jnp.sum(accs[3 * k + c], axis=0, keepdims=True)
                    mu_own[g, s + 1, b, row, :] = pol * (f0[g, b, row, :] + field)
            return none

        lax.fori_loop(0, nblk, block, 0)

    def force(g):
        chunks = BLOCK // R_FRC
        lane = lax.broadcasted_iota(jnp.int32, (R_FRC, BLOCK), 1)

        def block(b, none):
            own = mu_own[g, ITERS, b]
            mi = [
                [
                    jnp.broadcast_to(own[c * nb + k : c * nb + k + 1], (R_FRC, BLOCK))
                    for c in range(3)
                ]
                for k in range(nb)
            ]

            def chunk(m, accs):
                e = tiles_ref[b, m // chunks]
                start = pl.multiple_of((m % chunks) * R_FRC, R_FRC)
                col = col_m[g, e, pl.ds(start, R_FRC), :]
                qj = spread(col_p[e, pl.ds(start, R_FRC), :], 3 * beads)
                rows = pl.ds(pl.multiple_of(b * (NT * BLOCK) + m * R_FRC, R_FRC), R_FRC)
                out = []
                packed = jnp.zeros((R_FRC, BLOCK), jnp.float32)
                for k in range(nb):
                    bead = g * nb + k
                    mj = [spread(col, c * nb + k) for c in range(3)]
                    d = [geo[c, bead, rows, :] for c in range(3)]
                    b3 = geo[3, bead, rows, :]
                    half = 0.5 * geo[4, bead, rows, :]
                    a = mi[k][0] * d[0] + mi[k][1] * d[1] + mi[k][2] * d[2]
                    bb = mj[0] * d[0] + mj[1] * d[1] + mj[2] * d[2]
                    cc = mi[k][0] * mj[0] + mi[k][1] * mj[1] + mi[k][2] * mj[2]
                    lead = geo[5, bead, rows, :] * (qj * a - 0.5 * cc) + geo[6, bead, rows, :] * (
                        a * bb
                    )
                    ci = b3 * qj + half * bb
                    cj = half * a
                    for c in range(3):
                        f = d[c] * lead + ci * mi[k][c] + cj * mj[c]
                        out.append(accs[3 * k + c] + fold(f))
                        back = jnp.sum(f, axis=1, keepdims=True)
                        packed = jnp.where(lane == c * nb + k, back, packed)
                col_r[g, rows, :] = packed
                return tuple(out)

            zero = jnp.zeros((8, BLOCK), jnp.float32)
            accs = lax.fori_loop(0, NT * chunks, chunk, (zero,) * (3 * nb))
            for k in range(nb):
                for c in range(3):
                    f_own[g, b, c * nb + k : c * nb + k + 1, :] = jnp.sum(
                        accs[3 * k + c], axis=0, keepdims=True
                    )
            return none

        lax.fori_loop(0, nblk, block, 0)

        width = mu_own.shape[3]
        sums = [jnp.zeros((width, BLOCK), jnp.float32) for _ in range(3 * nblk)]
        for b in range(nblk):
            for t in range(NT):
                first = (b * NT + t) * BLOCK
                part = col_r[g, first : first + BLOCK, :].T[0:width]
                e = tiles_ref[b, t]
                for x in range(3 * nblk):
                    sums[x] = sums[x] + part * jnp.where(e == x, 1.0, 0.0)
        for b in range(nblk):
            r_send[g, 0, b] = sums[b]
            r_own[g, b] = sums[nblk + b]
            r_send[g, 1, b] = sums[2 * nblk + b]
        n = 2 * g
        return (
            send(r_send.at[g, 0], r_recv.at[g, 0], r_ss.at[n], r_rs.at[n], {"space": left}),
            send(
                r_send.at[g, 1], r_recv.at[g, 1], r_ss.at[n + 1], r_rs.at[n + 1], {"space": right}
            ),
        )

    moving = {}
    for g in range(GROUPS):
        geometry(g)
        moving[g] = mu_send(g, 0)
        heat_step()
    for s in range(ITERS):
        for g in range(GROUPS):
            mu_columns(g, s, moving[g])
            mutual(g, s)
            moving[g] = mu_send(g, s + 1)
            heat_step()
    back = {}
    for g in range(GROUPS):
        mu_columns(g, ITERS, moving[g])
        back[g] = force(g)
        heat_step()
    while heat_state["stage"] < len(partners):
        heat_step()

    bead_up.wait_recv()
    bead_down.wait_recv()
    total = jnp.sum(jnp.sum(k_own[len(partners)], axis=1, keepdims=True), axis=0, keepdims=True)
    kinetic = total / (3.0 * off_ref.shape[2] * ns * beads * nbd)
    scale = jnp.sqrt(1.0 + coupling * (target_temp / kinetic - 1.0))

    for g in range(GROUPS):
        for b in range(nblk):
            cut = slice(b * BLOCK, (b + 1) * BLOCK)
            for c in range(3):
                mu_out[c, g * nb : (g + 1) * nb, cut] = mu_own[g, ITERS, b, c * nb : (c + 1) * nb, :]
    for g in range(GROUPS):
        for copy in back[g]:
            copy.wait_recv()
        for b in range(nblk):
            cut = slice(b * BLOCK, (b + 1) * BLOCK)
            net = f_own[g, b] - (r_own[g, b] + r_recv[g, 0, b] + r_recv[g, 1, b])
            for c in range(3):
                force_out[c, g * nb : (g + 1) * nb, cut] = net[c * nb : (c + 1) * nb]
    inverse = time_step / mass_ref[0:1, :]
    for c in range(3):
        own = off_ref[c]
        before = jnp.concatenate([ob[0, c, beads - 1 : beads, :], own[: beads - 1]], axis=0)
        after = jnp.concatenate([own[1:], ob[1, c, 0:1, :]], axis=0)
        restoring = -bond_coef * (2.0 * own - before - after)
        new_velocity = scale * vel_ref[c] + (inverse * force_out[c] + time_step * restoring)
        vel_out[c] = new_velocity
        off_out[c] = own + time_step * new_velocity
    for copy in pending:
        copy.wait_send()


def per_device(ns, nbd, centroids, offsets, velocities, charges, polar, masses, groups, tiles):
    _, beads, atoms = offsets.shape
    nblk = atoms // BLOCK
    nb = beads // GROUPS
    width = -(-3 * nb // 8) * 8
    stages = (ns - 1).bit_length() + (nbd - 1).bit_length()
    vmem = pl.BlockSpec(memory_space=pltpu.VMEM)
    f32 = jnp.float32
    plane = nblk * NT * BLOCK
    dma = pltpu.SemaphoreType.DMA
    exchanges = 2 * GROUPS * (ITERS + 1)
    return pl.pallas_call(
        functools.partial(kernel, ns, nbd),
        out_shape=[jax.ShapeDtypeStruct(offsets.shape, f32)] * 4,
        in_specs=[vmem] * 7 + [pl.BlockSpec(memory_space=pltpu.SMEM)],
        out_specs=[vmem] * 4,
        scratch_shapes=[
            pltpu.VMEM((nblk, 3 * beads + 4, BLOCK), f32),
            pltpu.VMEM((2, nblk, 3 * beads + 4, BLOCK), f32),
            pltpu.VMEM((3 * nblk, BLOCK, 3 * beads + 4), f32),
            pltpu.VMEM((7, beads, plane, BLOCK), f32),
            pltpu.VMEM((GROUPS, nblk, width, BLOCK), f32),
            pltpu.VMEM((GROUPS, ITERS + 1, nblk, width, BLOCK), f32),
            pltpu.VMEM((GROUPS, ITERS + 1, 2, nblk, width, BLOCK), f32),
            pltpu.VMEM((GROUPS, 3 * nblk, BLOCK, width), f32),
            pltpu.VMEM((GROUPS, plane, BLOCK), f32),
            pltpu.VMEM((GROUPS, nblk, width, BLOCK), f32),
            pltpu.VMEM((GROUPS, 2, nblk, width, BLOCK), f32),
            pltpu.VMEM((GROUPS, 2, nblk, width, BLOCK), f32),
            pltpu.VMEM((GROUPS, nblk, width, BLOCK), f32),
            pltpu.VMEM((2,) + offsets.shape, f32),
            pltpu.VMEM((stages + 1, 8, BLOCK), f32),
            pltpu.VMEM((stages, 8, BLOCK), f32),
            dma((2,)),
            dma((2,)),
            dma((exchanges,)),
            dma((exchanges,)),
            dma((2 * GROUPS,)),
            dma((2 * GROUPS,)),
            dma((2,)),
            dma((2,)),
            dma((stages,)),
            dma((stages,)),
        ],
        compiler_params=pltpu.CompilerParams(collective_id=0, has_side_effects=True),
    )(
        centroids,
        offsets,
        velocities,
        charges.reshape(1, atoms),
        polar.reshape(1, atoms),
        masses.reshape(1, atoms),
        groups.reshape(1, atoms),
        tiles,
    )


def solution(mesh):
    ns, nbd = mesh.shape["space"], mesh.shape["bead"]
    assert ns > 4 and ns & (ns - 1) == 0 and nbd > 1 and nbd & (nbd - 1) == 0
    placed = (
        P(None, "space"),
        P(None, "bead", "space"),
        P(None, "bead", "space"),
        P("space"),
        P("space"),
        P("space"),
        P("space"),
        P("space", None),
    )
    return jax.shard_map(
        functools.partial(per_device, ns, nbd),
        mesh=mesh,
        in_specs=placed,
        out_specs=(P(None, "bead", "space"),) * 4,
        check_vma=False,
    )
```

time: 226 us -> 85.9 us (0.38)
  other arithmetic: 85.1 us -> 0 us
  Pallas kernels: 0 us -> 81.4 us
  blocking collectives: 38.9 us -> 0 us
  local copies, waits for them, and re-layouts: 37.1 us -> 3.34 us
  starting transfers between devices: 33.5 us -> 0 us
  loops' own time: 22.4 us -> 0 us
  waiting for transfers between devices: 4.82 us -> 0 us
    pallas_call x0 -> x1, Pallas kernels: none -> 81.4 us  [per_device(): pl.pallas_call(functools.partial(kernel, ns, nbd), out_shape=[jax.ShapeDt...]
    reduce_sum x29 -> x0, other arithmetic: 44.8 us -> none  [the longest x10 22.7 us: geometry(): square = jnp.sum(delta * delta, axis=0) + 1.0]
    psum x1 -> x0, blocking collectives: 38.9 us -> none  [per_device(): lax.psum(jnp.sum(masses[None, None, :] * velocities * velocities), ('spac...]
    ppermute x16 -> x0, starting transfers between devices: 33.5 us -> none  [the longest x7 27.7 us: extended(): after = lax.ppermute(first, axis, down)]
    gather x42 -> x0, local copies, waits for them, and re-layouts: 23.8 us -> none  [the longest x6 3.45 us: one(): mu_b[:, :, src].reshape(3, count, -1)]
    another operation x5 -> x0, loops' own time: 22.4 us -> none  [the longest x3 12.3 us: per_device(): mu = polar * (field0 + spread(lax.map(one, order)))]
    mul x13 -> x0, other arithmetic: 18.9 us -> none  [the longest x2 8.35 us: mutual(): inv_five * along]
    select_n x20 -> x0, other arithmetic: 7.74 us -> none  [the longest x6 4.14 us: one(): ext_b[:, :, src].reshape(3, count, -1)]
  transfers between devices with their start and end apart: 16 -> 0, of which waited for: 6 -> 0; matrix products, arithmetic and copies ran while one was open for 21% -> 0% of each run, Pallas kernels for 0% -> 0%
where the time goes in v1:
time: 85.9 us; the launch traced here: 85.4 us
  Pallas kernels  81.4 us (95%)
  local copies, waits for them, and re-layouts  3.34 us (4%)
    pallas_call x1, Pallas kernels, per_device(): pl.pallas_call(functools.partial(kernel, ns, nbd), out_shape=[jax.ShapeDt...  81.4 us
    unnamed x10, local copies, waits for them, and re-layouts  3.34 us

profile of v1, /device:TPU:0, one launch (start us, length us, event | category | flops | bytes accessed | tf_op | source)
XLA Modules:
  0.0 85.4 jit_solution(9063383779276597150)
XLA Ops:
  0.6 81.4 %shard_map.111 = (f32[3,4,256]{2,1,0:T(4,128)}, f32[3,4,256]{2,1,0:T(4,128)}, f32[3,4,256]{2,1,0:T(4,128)}, f32[3,4,256]{2,1,0:T(4,128)}) custom-call(f32[3,256]{1,0:T(4,128)} %cen_ref.1, f32[3,4,256]{2,1,0:T(4,128)} %off_ref.1, f32[3,4,256]{2,1,0:T(4,128)} %vel_ref.1, f32[1,256]{1,0:T(1,128)} %bitcast.4, f32[1,256]{1,0:T(1,128)} %bitcast.5, ...), custom_call_target="tpu_custom_call" | custom-call | tf_op jit(solution)/shard_map/pallas_call | solution.py:450
  82.1 0.0 copy-start.2
  82.1 1.3 %copy.16 = f32[3,4,256]{2,1,0:T(4,128)} copy(f32[3,4,256]{2,1,0:T(4,128)} %get-tuple-element.8) | data formatting | bytes 24576
  83.4 0.0 copy-done.2
  83.4 0.0 copy-start.1
  83.4 0.6 copy.17
  84.0 0.1 copy-done.1
  84.1 0.0 copy-start
  84.1 0.6 copy.18
  84.7 0.1 copy-done
  84.8 0.6 copy.19
Async XLA Ops:
  82.1 1.3 %copy-start.2 = (f32[3,4,256]{2,1,0:T(4,128)S(1)}, f32[3,4,256]{2,1,0:T(4,128)}, u32[]{:S(2)}) copy-start(f32[3,4,256]{2,1,0:T(4,128)} %get-tuple-element.9) | copy-start | bytes 36868
  83.4 0.7 copy-start.1
  84.1 0.7 copy-start

commit v2 on v1

--- a/solution.py
+++ b/solution.py
@@ -11,9 +11,9 @@
 NT = 4
 ITERS = 3
 GROUPS = 2
-R_GEO = 16
-R_MUT = 32
-R_FRC = 16
+R_GEO = 128
+R_MUT = 128
+R_FRC = 128
 
 slab_width = 9.0
 box_side = 24.0
@@ -59,11 +59,8 @@
     mu_own,
     mu_halo,
     col_m,
-    col_r,
-    r_own,
-    r_send,
-    r_recv,
     f_own,
+    slot_ref,
     ob,
     k_own,
     k_recv,
@@ -71,8 +68,6 @@
     p_rs,
     m_ss,
     m_rs,
-    r_ss,
-    r_rs,
     o_ss,
     o_rs,
     k_ss,
@@ -126,7 +121,23 @@
         p_own[b, base : base + 1, :] = chg_ref[0:1, cut]
         p_own[b, base + 1 : base + 2, :] = lax.rsqrt(pol_ref[0:1, cut])
         p_own[b, base + 2 : base + 3, :] = grp_ref[0:1, cut].astype(jnp.float32)
-        p_own[b, base + 3 : base + 4, :] = pol_ref[0:1, cut]
+        lane = lax.broadcasted_iota(jnp.int32, (1, BLOCK), 1)
+        flags = jnp.zeros((1, BLOCK), jnp.float32)
+        for t in range(NT):
+            flags = flags + jnp.where(lane == tiles_ref[b, t], 1.0, 0.0)
+            slot_ref[b, t] = tiles_ref[b, t]
+        p_own[b, base + 3 : base + 4, :] = flags
+        rank = 0
+        others = [0] * (3 * nblk - NT)
+        for e in range(3 * nblk):
+            free = 1
+            for t in range(NT):
+                free = jnp.where(tiles_ref[b, t] == e, 0, free)
+            for x in range(3 * nblk - NT):
+                others[x] = others[x] + jnp.where(rank == x, free * e, 0)
+            rank = rank + free
+        for x in range(3 * nblk - NT):
+            slot_ref[b, NT + x] = others[x]
     heat = jnp.zeros((beads, off_ref.shape[2]), jnp.float32)
     for c in range(3):
         heat = heat + vel_ref[c] * vel_ref[c]
@@ -179,7 +190,7 @@
             ).T
     heat_step()
 
-    def geometry(g):
+    def geometry(g, first, last, listed):
         chunks = BLOCK // R_GEO
 
         def block(b, none):
@@ -196,13 +207,13 @@
             ]
 
             def chunk(m, accs):
-                e = tiles_ref[b, m // chunks]
+                e = slot_ref[b, m // chunks]
                 start = pl.multiple_of((m % chunks) * R_GEO, R_GEO)
                 col = col_p[e, pl.ds(start, R_GEO), :]
                 qj = spread(col, 3 * beads)
                 kk = ki * spread(col, 3 * beads + 1)
                 mask = jnp.where(gi == spread(col, 3 * beads + 2), 0.0, 1.0)
-                rows = pl.ds(pl.multiple_of(b * (NT * BLOCK) + m * R_GEO, R_GEO), R_GEO)
+                rows = pl.ds(pl.multiple_of(b * (3 * nblk * BLOCK) + m * R_GEO, R_GEO), R_GEO)
                 out = []
                 for k in range(nb):
                     bead = g * nb + k
@@ -237,6 +248,8 @@
                     geo[4, bead, rows, :] = b5
                     geo[5, bead, rows, :] = d3
                     geo[6, bead, rows, :] = d5
+                    if not listed:
+                        continue
                     qb = qj * b3
                     out += [
                         accs[3 * k] + fold(qb * dx),
@@ -246,8 +259,12 @@
                 return tuple(out)
 
             zero = jnp.zeros((8, BLOCK), jnp.float32)
-            accs = lax.fori_loop(0, NT * chunks, chunk, (zero,) * (3 * nb))
-            pol = own[3 * beads + 3 : 3 * beads + 4]
+            accs = lax.fori_loop(
+                first * chunks, last * chunks, chunk, (zero,) * (3 * nb if listed else 0)
+            )
+            if not listed:
+                return none
+            pol = pol_ref[0:1, pl.ds(pl.multiple_of(b * BLOCK, BLOCK), BLOCK)]
             for k in range(nb):
                 for c in range(3):
                     field = jnp.sum(accs[3 * k + c], axis=0, keepdims=True)
@@ -282,7 +299,7 @@
                 e = tiles_ref[b, m // chunks]
                 start = pl.multiple_of((m % chunks) * R_MUT, R_MUT)
                 col = col_m[g, e, pl.ds(start, R_MUT), :]
-                rows = pl.ds(pl.multiple_of(b * (NT * BLOCK) + m * R_MUT, R_MUT), R_MUT)
+                rows = pl.ds(pl.multiple_of(b * (3 * nblk * BLOCK) + m * R_MUT, R_MUT), R_MUT)
                 out = []
                 for k in range(nb):
                     bead = g * nb + k
@@ -299,7 +316,7 @@
 
             zero = jnp.zeros((8, BLOCK), jnp.float32)
             accs = lax.fori_loop(0, NT * chunks, chunk, (zero,) * (3 * nb))
-            pol = p_own[b, 3 * beads + 3 : 3 * beads + 4, :]
+            pol = pol_ref[0:1, pl.ds(pl.multiple_of(b * BLOCK, BLOCK), BLOCK)]
             for k in range(nb):
                 for c in range(3):
                     row = slice(c * nb + k, c * nb + k + 1)
@@ -311,10 +328,10 @@
 
     def force(g):
         chunks = BLOCK // R_FRC
-        lane = lax.broadcasted_iota(jnp.int32, (R_FRC, BLOCK), 1)
 
         def block(b, none):
             own = mu_own[g, ITERS, b]
+            charge = p_own[b, 3 * beads : 3 * beads + 1, :]
             mi = [
                 [
                     jnp.broadcast_to(own[c * nb + k : c * nb + k + 1], (R_FRC, BLOCK))
@@ -324,37 +341,43 @@
             ]
 
             def chunk(m, accs):
-                e = tiles_ref[b, m // chunks]
+                slot = m // chunks
+                e = slot_ref[b, slot]
                 start = pl.multiple_of((m % chunks) * R_FRC, R_FRC)
                 col = col_m[g, e, pl.ds(start, R_FRC), :]
-                qj = spread(col_p[e, pl.ds(start, R_FRC), :], 3 * beads)
-                rows = pl.ds(pl.multiple_of(b * (NT * BLOCK) + m * R_FRC, R_FRC), R_FRC)
+                mine = (2 - e // nblk) * nblk + b
+                full = (R_FRC, BLOCK)
+                given = jnp.where(slot < NT, 1.0, 0.0)
+                taken = jnp.broadcast_to(
+                    col_p[e, pl.ds(mine, 1), 3 * beads + 3 : 3 * beads + 4], (1, BLOCK)
+                )
+                qj = spread(col_p[e, pl.ds(start, R_FRC), :], 3 * beads) * given
+                qi = jnp.broadcast_to(charge * taken, full)
+                both = jnp.broadcast_to(taken + given, full)
+                half = 0.5 * both
+                rows = pl.ds(pl.multiple_of(b * (3 * nblk * BLOCK) + m * R_FRC, R_FRC), R_FRC)
                 out = []
-                packed = jnp.zeros((R_FRC, BLOCK), jnp.float32)
                 for k in range(nb):
                     bead = g * nb + k
                     mj = [spread(col, c * nb + k) for c in range(3)]
                     d = [geo[c, bead, rows, :] for c in range(3)]
                     b3 = geo[3, bead, rows, :]
-                    half = 0.5 * geo[4, bead, rows, :]
+                    hb = half * geo[4, bead, rows, :]
                     a = mi[k][0] * d[0] + mi[k][1] * d[1] + mi[k][2] * d[2]
                     bb = mj[0] * d[0] + mj[1] * d[1] + mj[2] * d[2]
                     cc = mi[k][0] * mj[0] + mi[k][1] * mj[1] + mi[k][2] * mj[2]
-                    lead = geo[5, bead, rows, :] * (qj * a - 0.5 * cc) + geo[6, bead, rows, :] * (
-                        a * bb
-                    )
-                    ci = b3 * qj + half * bb
-                    cj = half * a
+                    lead = geo[5, bead, rows, :] * (qj * a - qi * bb - half * cc) + geo[
+                        6, bead, rows, :
+                    ] * (both * (a * bb))
+                    ci = b3 * qj + hb * bb
+                    cj = hb * a - b3 * qi
                     for c in range(3):
                         f = d[c] * lead + ci * mi[k][c] + cj * mj[c]
                         out.append(accs[3 * k + c] + fold(f))
-                        back = jnp.sum(f, axis=1, keepdims=True)
-                        packed = jnp.where(lane == c * nb + k, back, packed)
-                col_r[g, rows, :] = packed
                 return tuple(out)
 
             zero = jnp.zeros((8, BLOCK), jnp.float32)
-            accs = lax.fori_loop(0, NT * chunks, chunk, (zero,) * (3 * nb))
+            accs = lax.fori_loop(0, 3 * nblk * chunks, chunk, (zero,) * (3 * nb))
             for k in range(nb):
                 for c in range(3):
                     f_own[g, b, c * nb + k : c * nb + k + 1, :] = jnp.sum(
@@ -364,30 +387,9 @@
 
         lax.fori_loop(0, nblk, block, 0)
 
-        width = mu_own.shape[3]
-        sums = [jnp.zeros((width, BLOCK), jnp.float32) for _ in range(3 * nblk)]
-        for b in range(nblk):
-            for t in range(NT):
-                first = (b * NT + t) * BLOCK
-                part = col_r[g, first : first + BLOCK, :].T[0:width]
-                e = tiles_ref[b, t]
-                for x in range(3 * nblk):
-                    sums[x] = sums[x] + part * jnp.where(e == x, 1.0, 0.0)
-        for b in range(nblk):
-            r_send[g, 0, b] = sums[b]
-            r_own[g, b] = sums[nblk + b]
-            r_send[g, 1, b] = sums[2 * nblk + b]
-        n = 2 * g
-        return (
-            send(r_send.at[g, 0], r_recv.at[g, 0], r_ss.at[n], r_rs.at[n], {"space": left}),
-            send(
-                r_send.at[g, 1], r_recv.at[g, 1], r_ss.at[n + 1], r_rs.at[n + 1], {"space": right}
-            ),
-        )
-
     moving = {}
     for g in range(GROUPS):
-        geometry(g)
+        geometry(g, 0, NT, True)
         moving[g] = mu_send(g, 0)
         heat_step()
     for s in range(ITERS):
@@ -396,10 +398,11 @@
             mutual(g, s)
             moving[g] = mu_send(g, s + 1)
             heat_step()
-    back = {}
+        for g in range(s, GROUPS, ITERS):
+            geometry(g, NT, 3 * nblk, False)
     for g in range(GROUPS):
         mu_columns(g, ITERS, moving[g])
-        back[g] = force(g)
+        force(g)
         heat_step()
     while heat_state["stage"] < len(partners):
         heat_step()
@@ -416,11 +419,9 @@
             for c in range(3):
                 mu_out[c, g * nb : (g + 1) * nb, cut] = mu_own[g, ITERS, b, c * nb : (c + 1) * nb, :]
     for g in range(GROUPS):
-        for copy in back[g]:
-            copy.wait_recv()
         for b in range(nblk):
             cut = slice(b * BLOCK, (b + 1) * BLOCK)
-            net = f_own[g, b] - (r_own[g, b] + r_recv[g, 0, b] + r_recv[g, 1, b])
+            net = f_own[g, b]
             for c in range(3):
                 force_out[c, g * nb : (g + 1) * nb, cut] = net[c * nb : (c + 1) * nb]
     inverse = time_step / mass_ref[0:1, :]
@@ -444,7 +445,7 @@
     stages = (ns - 1).bit_length() + (nbd - 1).bit_length()
     vmem = pl.BlockSpec(memory_space=pltpu.VMEM)
     f32 = jnp.float32
-    plane = nblk * NT * BLOCK
+    plane = nblk * 3 * nblk * BLOCK
     dma = pltpu.SemaphoreType.DMA
     exchanges = 2 * GROUPS * (ITERS + 1)
     return pl.pallas_call(
@@ -461,11 +462,8 @@
             pltpu.VMEM((GROUPS, ITERS + 1, nblk, width, BLOCK), f32),
             pltpu.VMEM((GROUPS, ITERS + 1, 2, nblk, width, BLOCK), f32),
             pltpu.VMEM((GROUPS, 3 * nblk, BLOCK, width), f32),
-            pltpu.VMEM((GROUPS, plane, BLOCK), f32),
             pltpu.VMEM((GROUPS, nblk, width, BLOCK), f32),
-            pltpu.VMEM((GROUPS, 2, nblk, width, BLOCK), f32),
-            pltpu.VMEM((GROUPS, 2, nblk, width, BLOCK), f32),
-            pltpu.VMEM((GROUPS, nblk, width, BLOCK), f32),
+            pltpu.SMEM((nblk, 3 * nblk), jnp.int32),
             pltpu.VMEM((2,) + offsets.shape, f32),
             pltpu.VMEM((stages + 1, 8, BLOCK), f32),
             pltpu.VMEM((stages, 8, BLOCK), f32),
@@ -473,8 +471,6 @@
             dma((2,)),
             dma((exchanges,)),
             dma((exchanges,)),
-            dma((2 * GROUPS,)),
-            dma((2 * GROUPS,)),
             dma((2,)),
             dma((2,)),
             dma((stages,)),

time: 85.9 us -> 48.3 us (0.56)
  Pallas kernels: 81.4 us -> 43.8 us
    pallas_call x1, Pallas kernels: 81.4 us -> 43.8 us  [per_device(): pl.pallas_call(functools.partial(kernel, ns, nbd), out_shape=[jax.ShapeDt...]
where the time goes in v2:
time: 48.3 us; the launch traced here: 47.8 us
  Pallas kernels  43.8 us (91%)
  local copies, waits for them, and re-layouts  3.34 us (7%)
  between operations  0.65 us (1%)
    pallas_call x1, Pallas kernels, per_device(): pl.pallas_call(functools.partial(kernel, ns, nbd), out_shape=[jax.ShapeDt...  43.8 us
    unnamed x10, local copies, waits for them, and re-layouts  3.34 us

profile of v2, /device:TPU:0, one launch (start us, length us, event | category | flops | bytes accessed | tf_op | source)
XLA Modules:
  0.0 47.8 jit_solution(1869872712273891153)
XLA Ops:
  0.6 43.8 %shard_map.111 = (f32[3,4,256]{2,1,0:T(4,128)}, f32[3,4,256]{2,1,0:T(4,128)}, f32[3,4,256]{2,1,0:T(4,128)}, f32[3,4,256]{2,1,0:T(4,128)}) custom-call(f32[3,256]{1,0:T(4,128)} %cen_ref.1, f32[3,4,256]{2,1,0:T(4,128)} %off_ref.1, f32[3,4,256]{2,1,0:T(4,128)} %vel_ref.1, f32[1,256]{1,0:T(1,128)} %bitcast.4, f32[1,256]{1,0:T(1,128)} %bitcast.5, ...), custom_call_target="tpu_custom_call" | custom-call | tf_op jit(solution)/shard_map/pallas_call | solution.py:451
  44.5 0.0 copy-start.2
  44.5 1.3 %copy.16 = f32[3,4,256]{2,1,0:T(4,128)} copy(f32[3,4,256]{2,1,0:T(4,128)} %get-tuple-element.8) | data formatting | bytes 24576
  45.8 0.0 copy-done.2
  45.8 0.0 copy-start.1
  45.8 0.6 %copy.17 = f32[3,4,256]{2,1,0:T(4,128)} copy(f32[3,4,256]{2,1,0:T(4,128)S(1)} %copy-done.2) | data formatting | bytes 24576
  46.4 0.1 copy-done.1
  46.5 0.0 copy-start
  46.5 0.6 %copy.18 = f32[3,4,256]{2,1,0:T(4,128)} copy(f32[3,4,256]{2,1,0:T(4,128)S(1)} %copy-done.1) | data formatting | bytes 24576
  47.1 0.1 copy-done
  47.2 0.6 %copy.19 = f32[3,4,256]{2,1,0:T(4,128)} copy(f32[3,4,256]{2,1,0:T(4,128)S(1)} %copy-done) | data formatting | bytes 24576
Async XLA Ops:
  44.5 1.3 %copy-start.2 = (f32[3,4,256]{2,1,0:T(4,128)S(1)}, f32[3,4,256]{2,1,0:T(4,128)}, u32[]{:S(2)}) copy-start(f32[3,4,256]{2,1,0:T(4,128)} %get-tuple-element.9) | copy-start | bytes 36868
  45.8 0.7 %copy-start.1 = (f32[3,4,256]{2,1,0:T(4,128)S(1)}, f32[3,4,256]{2,1,0:T(4,128)}, u32[]{:S(2)}) copy-start(f32[3,4,256]{2,1,0:T(4,128)} %get-tuple-element.10) | copy-start | bytes 36868
  46.5 0.7 %copy-start = (f32[3,4,256]{2,1,0:T(4,128)S(1)}, f32[3,4,256]{2,1,0:T(4,128)}, u32[]{:S(2)}) copy-start(f32[3,4,256]{2,1,0:T(4,128)} %get-tuple-element.11) | copy-start | bytes 36868

commit v3 on v2

--- a/solution.py
+++ b/solution.py
@@ -23,6 +23,7 @@
 time_step = 0.05
 target_temp = 8.0
 coupling = 0.5
+log2_e = 1.4426950408889634
 
 
 def spread(col, k):
@@ -58,7 +59,7 @@
     f0,
     mu_own,
     mu_halo,
-    col_m,
+    wide_m,
     f_own,
     slot_ref,
     ob,
@@ -190,7 +191,7 @@
             ).T
     heat_step()
 
-    def geometry(g, first, last, listed):
+    def geometry(g, first, last, listed, start, stop):
         chunks = BLOCK // R_GEO
 
         def block(b, none):
@@ -208,11 +209,11 @@
 
             def chunk(m, accs):
                 e = slot_ref[b, m // chunks]
-                start = pl.multiple_of((m % chunks) * R_GEO, R_GEO)
-                col = col_p[e, pl.ds(start, R_GEO), :]
+                low = pl.multiple_of((m % chunks) * R_GEO, R_GEO)
+                col = col_p[e, pl.ds(low, R_GEO), :]
                 qj = spread(col, 3 * beads)
                 kk = ki * spread(col, 3 * beads + 1)
-                mask = jnp.where(gi == spread(col, 3 * beads + 2), 0.0, 1.0)
+                mask = jnp.where(gi == spread(col, 3 * beads + 2), 0.0, cut_square**-2)
                 rows = pl.ds(pl.multiple_of(b * (3 * nblk * BLOCK) + m * R_GEO, R_GEO), R_GEO)
                 out = []
                 for k in range(nb):
@@ -226,21 +227,19 @@
                     r = lax.rsqrt(s)
                     r2 = r * r
                     u = kk * (s * s * r)
-                    fade = jnp.exp(-u)
+                    fade = jnp.exp2(u * -log2_e)
                     ue = u * fade
                     l3 = 1.0 - fade
                     l5 = l3 - ue
-                    t = jnp.maximum(1.0 - s * (1.0 / cut_square), 0.0)
-                    tm = t * mask
-                    w = tm * t
-                    r3 = r2 * r
-                    wr3 = w * r3
+                    t = jnp.maximum(cut_square - s, 0.0)
+                    p = t * mask * (r2 * r)
+                    wr3 = p * t
                     b3 = wr3 * l3
-                    wr5 = wr3 * r2 * 3.0
-                    b5 = wr5 * l5
-                    slope = tm * r3 * (-2.0 / cut_square)
-                    d3 = 2.0 * slope * l3 + 3.0 * (wr3 * r2) * (ue - l3)
-                    d5 = r2 * (3.0 * slope * l5 + wr5 * (1.5 * u * ue - 2.5 * l5))
+                    h3 = 3.0 * (wr3 * r2)
+                    b5 = h3 * l5
+                    p4 = -4.0 * p
+                    d3 = p4 * l3 - b5
+                    d5 = r2 * (p4 * l5 + h3 * (u * ue) - (5.0 / 3.0) * b5)
                     geo[0, bead, rows, :] = dx
                     geo[1, bead, rows, :] = dy
                     geo[2, bead, rows, :] = dz
@@ -272,7 +271,7 @@
                     mu_own[g, 0, b, c * nb + k : c * nb + k + 1, :] = pol * field
             return none
 
-        lax.fori_loop(0, nblk, block, 0)
+        lax.fori_loop(start, stop, block, 0)
 
     def mu_send(g, s):
         n = 2 * (g * (ITERS + 1) + s)
@@ -283,13 +282,18 @@
             ),
         )
 
+    def widen(g, e, rows):
+        col = rows.T
+        for k in range(3 * nb):
+            wide_m[g, e, k] = spread(col, k)
+
     def mu_columns(g, s, copies):
         for b in range(nblk):
-            col_m[g, nblk + b] = mu_own[g, s, b].T
+            widen(g, nblk + b, mu_own[g, s, b])
         for d in range(2):
             copies[d].wait_recv()
             for b in range(nblk):
-                col_m[g, 2 * d * nblk + b] = mu_halo[g, s, d, b].T
+                widen(g, 2 * d * nblk + b, mu_halo[g, s, d, b])
 
     def mutual(g, s):
         chunks = BLOCK // R_MUT
@@ -298,12 +302,11 @@
             def chunk(m, accs):
                 e = tiles_ref[b, m // chunks]
                 start = pl.multiple_of((m % chunks) * R_MUT, R_MUT)
-                col = col_m[g, e, pl.ds(start, R_MUT), :]
                 rows = pl.ds(pl.multiple_of(b * (3 * nblk * BLOCK) + m * R_MUT, R_MUT), R_MUT)
                 out = []
                 for k in range(nb):
                     bead = g * nb + k
-                    mx, my, mz = (spread(col, k), spread(col, nb + k), spread(col, 2 * nb + k))
+                    mx, my, mz = (wide_m[g, e, c * nb + k, pl.ds(start, R_MUT), :] for c in range(3))
                     dx, dy, dz = (geo[0, bead, rows, :], geo[1, bead, rows, :], geo[2, bead, rows, :])
                     b3 = geo[3, bead, rows, :]
                     along = geo[4, bead, rows, :] * (dx * mx + dy * my + dz * mz)
@@ -344,7 +347,6 @@
                 slot = m // chunks
                 e = slot_ref[b, slot]
                 start = pl.multiple_of((m % chunks) * R_FRC, R_FRC)
-                col = col_m[g, e, pl.ds(start, R_FRC), :]
                 mine = (2 - e // nblk) * nblk + b
                 full = (R_FRC, BLOCK)
                 given = jnp.where(slot < NT, 1.0, 0.0)
@@ -355,11 +357,12 @@
                 qi = jnp.broadcast_to(charge * taken, full)
                 both = jnp.broadcast_to(taken + given, full)
                 half = 0.5 * both
+                steep = 1.5 * both
                 rows = pl.ds(pl.multiple_of(b * (3 * nblk * BLOCK) + m * R_FRC, R_FRC), R_FRC)
                 out = []
                 for k in range(nb):
                     bead = g * nb + k
-                    mj = [spread(col, c * nb + k) for c in range(3)]
+                    mj = [wide_m[g, e, c * nb + k, pl.ds(start, R_FRC), :] for c in range(3)]
                     d = [geo[c, bead, rows, :] for c in range(3)]
                     b3 = geo[3, bead, rows, :]
                     hb = half * geo[4, bead, rows, :]
@@ -368,7 +371,7 @@
                     cc = mi[k][0] * mj[0] + mi[k][1] * mj[1] + mi[k][2] * mj[2]
                     lead = geo[5, bead, rows, :] * (qj * a - qi * bb - half * cc) + geo[
                         6, bead, rows, :
-                    ] * (both * (a * bb))
+                    ] * (steep * (a * bb))
                     ci = b3 * qj + hb * bb
                     cj = hb * a - b3 * qi
                     for c in range(3):
@@ -387,19 +390,28 @@
 
         lax.fori_loop(0, nblk, block, 0)
 
+    rest = [(g, b) for g in range(GROUPS) for b in range(nblk)]
+
+    def fill():
+        if rest:
+            g, b = rest.pop(0)
+            geometry(g, NT, 3 * nblk, False, b, b + 1)
+
     moving = {}
     for g in range(GROUPS):
-        geometry(g, 0, NT, True)
+        geometry(g, 0, NT, True, 0, nblk)
         moving[g] = mu_send(g, 0)
         heat_step()
+    fill()
     for s in range(ITERS):
         for g in range(GROUPS):
             mu_columns(g, s, moving[g])
             mutual(g, s)
             moving[g] = mu_send(g, s + 1)
             heat_step()
-        for g in range(s, GROUPS, ITERS):
-            geometry(g, NT, 3 * nblk, False)
+        fill()
+    while rest:
+        fill()
     for g in range(GROUPS):
         mu_columns(g, ITERS, moving[g])
         force(g)
@@ -437,6 +449,17 @@
         copy.wait_send()
 
 
+def relay(*refs):
+    count = (len(refs) - 1) // 2
+    copies = [
+        pltpu.make_async_copy(refs[i], refs[count + i], refs[-1].at[i]) for i in range(count)
+    ]
+    for copy in copies:
+        copy.start()
+    for copy in copies:
+        copy.wait()
+
+
 def per_device(ns, nbd, centroids, offsets, velocities, charges, polar, masses, groups, tiles):
     _, beads, atoms = offsets.shape
     nblk = atoms // BLOCK
@@ -448,7 +471,7 @@
     plane = nblk * 3 * nblk * BLOCK
     dma = pltpu.SemaphoreType.DMA
     exchanges = 2 * GROUPS * (ITERS + 1)
-    return pl.pallas_call(
+    results = pl.pallas_call(
         functools.partial(kernel, ns, nbd),
         out_shape=[jax.ShapeDtypeStruct(offsets.shape, f32)] * 4,
         in_specs=[vmem] * 7 + [pl.BlockSpec(memory_space=pltpu.SMEM)],
@@ -461,7 +484,7 @@
             pltpu.VMEM((GROUPS, nblk, width, BLOCK), f32),
             pltpu.VMEM((GROUPS, ITERS + 1, nblk, width, BLOCK), f32),
             pltpu.VMEM((GROUPS, ITERS + 1, 2, nblk, width, BLOCK), f32),
-            pltpu.VMEM((GROUPS, 3 * nblk, BLOCK, width), f32),
+            pltpu.VMEM((GROUPS, 3 * nblk, 3 * nb, BLOCK, BLOCK), f32),
             pltpu.VMEM((GROUPS, nblk, width, BLOCK), f32),
             pltpu.SMEM((nblk, 3 * nblk), jnp.int32),
             pltpu.VMEM((2,) + offsets.shape, f32),
@@ -487,6 +510,14 @@
         groups.reshape(1, atoms),
         tiles,
     )
+    anywhere = pl.BlockSpec(memory_space=pl.ANY)
+    return pl.pallas_call(
+        relay,
+        out_shape=[jax.ShapeDtypeStruct(offsets.shape, f32)] * 4,
+        in_specs=[anywhere] * 4,
+        out_specs=[anywhere] * 4,
+        scratch_shapes=[dma((4,))],
+    )(*results)
 
 
 def solution(mesh):

time: 48.3 us -> 45 us (0.932)
  local copies, waits for them, and re-layouts: 3.34 us -> 0 us
    unnamed x10 -> x0, local copies, waits for them, and re-layouts: 3.34 us -> none
    pallas_call x0 -> x1, Pallas kernels: none -> 2.63 us  [per_device(): pl.pallas_call(relay, out_shape=[jax.ShapeDtypeStruct(offsets.shape, f32)...]
    pallas_call x1, Pallas kernels: 43.8 us -> 41.5 us  [per_device(): pl.pallas_call(functools.partial(kernel, ns, nbd), out_shape=[jax.ShapeDt...]
where the time goes in v3:
time: 45 us; the launch traced here: 44.8 us
  Pallas kernels  44.2 us (98%)
  between operations  0.64 us (1%)
    pallas_call x1, Pallas kernels, per_device(): pl.pallas_call(functools.partial(kernel, ns, nbd), out_shape=[jax.ShapeDt...  41.5 us
    pallas_call x1, Pallas kernels, per_device(): pl.pallas_call(relay, out_shape=[jax.ShapeDtypeStruct(offsets.shape, f32)...  2.63 us

profile of v3, /device:TPU:0, one launch (start us, length us, event | category | flops | bytes accessed | tf_op | source)
XLA Modules:
  0.0 44.8 jit_solution(6775590279782646021)
XLA Ops:
  0.6 41.5 %shard_map.111 = (f32[3,4,256]{2,1,0:T(4,128)}, f32[3,4,256]{2,1,0:T(4,128)}, f32[3,4,256]{2,1,0:T(4,128)}, f32[3,4,256]{2,1,0:T(4,128)}) custom-call(f32[3,256]{1,0:T(4,128)} %cen_ref.1, f32[3,4,256]{2,1,0:T(4,128)} %off_ref.1, f32[3,4,256]{2,1,0:T(4,128)} %vel_ref.1, f32[1,256]{1,0:T(1,128)} %bitcast.4, f32[1,256]{1,0:T(1,128)} %bitcast.5, ...), custom_call_target="tpu_custom_call" | custom-call | tf_op jit(solution)/shard_map/pallas_call | solution.py:474
  42.2 2.6 %shard_map.112 = (f32[3,4,256]{2,1,0:T(4,128)}, f32[3,4,256]{2,1,0:T(4,128)}, f32[3,4,256]{2,1,0:T(4,128)}, f32[3,4,256]{2,1,0:T(4,128)}) custom-call(f32[3,4,256]{2,1,0:T(4,128)} %get-tuple-element.8.refs_0_, f32[3,4,256]{2,1,0:T(4,128)} %get-tuple-element.9.refs_1_, f32[3,4,256]{2,1,0:T(4,128)} %get-tuple-element.10.refs_2_, ...), custom_call_target="tpu_custom_call" | custom-call | tf_op jit(solution)/shard_map/pallas_call | solution.py:514
